TPU v7x, 32 devices: a whole 2x2x4 slice. The times are simulated.
32 devices in a mesh: freq: 2 (over y), slab: 16 (over z, x, core).
Axes of the slice: x: 2, y: 2, z: 4, core: 2. Of those that a mesh axis runs over, the one named last changes fastest.
Arguments:
- wavefield: float32 [2, 2, 2048, 2048], P(None, 'freq', 'slab'), may hold values from -6 to 6
- freqs: float32 [2], P('freq'), may hold values from 0.15 to 0.45
- velocity: float32 [3, 2048, 2048], P(None, 'slab', 'freq'), may hold values from 0.7 to 1.6
- ref_slow: float32 [3, 2], replicated, may hold values from 0.6 to 1.5, as said below
Outputs:
- migrated: float32 [2, 2, 2048, 2048], P(None, 'freq', 'slab')
Inputs may be any that keep to these rules, and one draw needn't show every extreme that they name: ref_slow[d, 1] - ref_slow[d, 0] lies between 0.3 and 0.6 for every depth step.
All inputs are finite; a program needn't handle non-finite values.
Results may differ from a plain program's by a relative error of at most 0.0003.
Values sent between devices are 32-bit elements; how exact they have to be, the bound alone decides.
A program may use at most 64 MiB of HBM per device.

v0:
```python
import math
import jax
import jax.numpy as jnp
from jax import lax
from jax.sharding import PartitionSpec as P

two_pi = 2.0 * math.pi
depth_step = 2.0


def dft_matrix(length, sign):
    index = jnp.arange(length, dtype=jnp.int32)
    product = index[:, None] * index[None, :] % length
    angle = sign * two_pi / length * product.astype(jnp.float32)
    scale = 1.0 / math.sqrt(length)
    return (jnp.cos(angle) * scale, jnp.sin(angle) * scale)


def twiddle(outer, inner, sign):
    length = outer * inner
    product = (
        jnp.arange(outer, dtype=jnp.int32)[:, None]
        * jnp.arange(inner, dtype=jnp.int32)[None, :]
        % length
    )
    angle = sign * two_pi / length * product.astype(jnp.float32)
    return (jnp.cos(angle), jnp.sin(angle))


def complex_mix(form, mat_real, mat_imag, data_real, data_imag):

    def product(matrix, data):
        return jnp.einsum(form, matrix, data, precision=lax.Precision.HIGHEST)

    return (
        product(mat_real, data_real) - product(mat_imag, data_imag),
        product(mat_real, data_imag) + product(mat_imag, data_real),
    )


def transform(real, imag, trailing, sign):
    length = real.shape[-2] if trailing else real.shape[-1]
    inner = min(length, 128)
    outer = length // inner
    outer_real, outer_imag = dft_matrix(outer, sign)
    inner_real, inner_imag = dft_matrix(inner, sign)
    turn_real, turn_imag = twiddle(outer, inner, sign)
    if trailing:
        leading = real.shape[:-2]
        tail = real.shape[-1:]
        form_outer = "ka,...abm->...kbm"
        form_inner = "bj,...kbm->...kjm"
        turn_real = turn_real[:, :, None]
        turn_imag = turn_imag[:, :, None]
    else:
        leading = real.shape[:-1]
        tail = ()
        form_outer = "ka,...ab->...kb"
        form_inner = "bj,...kb->...kj"
    split_shape = leading + (outer, inner) + tail
    real = real.reshape(split_shape)
    imag = imag.reshape(split_shape)
    if sign < 0:
        real, imag = complex_mix(form_outer, outer_real, outer_imag, real, imag)
        real, imag = (real * turn_real - imag * turn_imag, real * turn_imag + imag * turn_real)
        real, imag = complex_mix(form_inner, inner_real, inner_imag, real, imag)
    else:
        real, imag = complex_mix(form_inner, inner_real, inner_imag, real, imag)
        real, imag = (real * turn_real - imag * turn_imag, real * turn_imag + imag * turn_real)
        real, imag = complex_mix(form_outer, outer_real, outer_imag, real, imag)
    joined = leading + (length,) + tail
    return (real.reshape(joined), imag.reshape(joined))


def wave_numbers(positions, length):
    inner = min(length, 128)
    outer = length // inner
    number = positions // inner + outer * (positions % inner)
    number = jnp.where(number < length // 2, number, number - length)
    return number.astype(jnp.float32) / length


def forward_x(items):
    real, imag = transform(items[0], items[1], True, -1)
    return jnp.stack((real, imag))


def inverse_y(items):
    real, imag = transform(items[:, 0], items[:, 1], False, 1)
    return jnp.stack((real, imag), axis=1)


def shards(wavefield, freqs, velocity, ref_slow):
    slabs = lax.axis_size("slab")
    slab_index = lax.axis_index("slab")
    rows = wavefield.shape[2]
    width_x = rows * slabs
    width_y = wavefield.shape[3]
    columns = width_y // slabs
    depth = ref_slow.shape[0]
    along_x = wave_numbers(jnp.arange(width_x, dtype=jnp.int32), width_x)
    along_y = wave_numbers(slab_index * columns + jnp.arange(columns, dtype=jnp.int32), width_y)
    square = along_x[:, None] ** 2 + along_y[None, :] ** 2
    freq_col = freqs[:, None, None]

    def advance(level, field):
        local_tile = lax.dynamic_index_in_dim(velocity, level, 0, keepdims=False)
        tile = lax.all_gather(local_tile, "freq", axis=1, tiled=True)
        real, imag = transform(field[0], field[1], False, -1)
        spectrum = forward_x(
            lax.all_to_all(jnp.stack((real, imag)), "slab", split_axis=3, concat_axis=2, tiled=True)
        )
        slow_pair = lax.dynamic_index_in_dim(ref_slow, level, 0, keepdims=False)
        slowness = 1.0 / tile
        upper_weight = jnp.clip((slowness - slow_pair[0]) / (slow_pair[1] - slow_pair[0]), 0.0, 1.0)
        weights = [1.0 - upper_weight, upper_weight]
        shifted = []
        for branch in range(2):
            target = (freq_col * slow_pair[branch]) ** 2 - square[None]
            angle = two_pi * depth_step * jnp.sqrt(jnp.abs(target))
            live = target >= 0
            prop_real = jnp.where(live, jnp.cos(angle), jnp.exp(-angle))
            prop_imag = jnp.where(live, jnp.sin(angle), jnp.zeros_like(angle))
            spec_real = spectrum[0] * prop_real - spectrum[1] * prop_imag
            spec_imag = spectrum[0] * prop_imag + spectrum[1] * prop_real
            back_real, back_imag = transform(spec_real, spec_imag, True, 1)
            shifted.append(jnp.stack((back_real, back_imag)))
        pieces = []
        for branch in range(2):
            moved = lax.all_to_all(shifted[branch], "slab", split_axis=2, concat_axis=3, tiled=True)
            pieces.append(inverse_y(moved[None])[0])
        spatial = jnp.stack(pieces)
        new_real = jnp.zeros_like(field[0])
        new_imag = jnp.zeros_like(field[1])
        for branch in range(2):
            theta = two_pi * depth_step * freq_col * (slowness - slow_pair[branch])[None]
            weight = weights[branch][None]
            cosine = jnp.cos(theta)
            sine = jnp.sin(theta)
            part_real = spatial[branch, 0]
            part_imag = spatial[branch, 1]
            new_real = new_real + weight * (cosine * part_real - sine * part_imag)
            new_imag = new_imag + weight * (cosine * part_imag + sine * part_real)
        return jnp.stack((new_real, new_imag))

    return lax.fori_loop(0, depth, advance, wavefield)


def solution(mesh):
    return jax.shard_map(
        shards,
        mesh=mesh,
        in_specs=(P(None, "freq", "slab", None), P("freq"), P(None, "slab", "freq"), P()),
        out_specs=P(None, "freq", "slab", None),
        check_vma=False,
    )
```

profile of v0, /device:TPU:11, one launch (start us, length us, event | category | flops | bytes accessed | tf_op | source)
XLA Modules:
  0.0 790.6 jit_solution(8718204456309350147)
XLA Ops:
  8.1 774.4 %while.17 = (s32[]{:T(128)}, f32[2,1,128,2048]{3,2,1,0:T(8,128)S(1)}, f32[3,128,1024]{2,1,0:T(8,128)}, f32[3,2]{0,1:T(2,128)S(1)}, f32[1,1,1]{2,1,0:T(1,128)}, /...) while((s32[]{:T(128)}, f32[2,1,128,2048]{3,2,1,0:T(8,128)S(1)}, ...), condition=%wide.region_1.2_spmd.clone, body=%wide.region_0.1_spmd.clone.sunk | while | flops 10909407232 | bytes 317449280 | solution.py:146
  23.0 6.5 all-to-all-start
  32.9 10.2 %fusion.669 = (f32[2048,128]{1,0:T(8,128)}, f32[2048,128]{1,0:T(8,128)}, f32[2048,128]{1,0:T(8,128)S(1)}, f32[2048,128]{1,0:T(8,128)}) fusion(f32[128]{0:T(128)S(1)} %get-tuple-element.413, f32[2048]{0:T(1024)S(1)} %get-tuple-element.414, f32[]{:T(128)} %bitcast.650, f32[]{:T(128)} %bitcast.652), kind=kLoop, calls=%fused_computation.62.clone.1 | loop fusion | flops 3932160 | bytes 4203016 | tf_op jit(solution)/shard_map/while/body/eval_jaxpr/jit(_where)/select_n | solution.py:123
  52.1 24.8 %all-to-all-done = f32[2,1,128,2048]{2,1,0,3:T(1,128)S(1)} async-done(((f32[2,1,128,2048]{2,1,0,3:T(1,128)}), f32[2,1,128,2048]{2,1,0,3:T(1,128)S(1)}, u32[]{:S(2)}, u32[]{:S(2)}) %all-to-all-start) | async-done | bytes 2097184 | tf_op jit(solution)/shard_map/while/body/eval_jaxpr/all_to_all | solution.py:111
  114.7 10.2 %copy.403 = f32[2,1,2048,128]{3,1,0,2:T(1,128)} copy(f32[2,1,2048,128]{3,2,1,0:T(8,128)S(1)} %pad_maximum_fusion.10) | data formatting | bytes 4194304 | tf_op jit(solution)/shard_map/while/body/eval_jaxpr/stack | solution.py:127
  136.0 10.0 %copy.396 = f32[2,1,2048,128]{3,1,0,2:T(1,128)} copy(f32[2,1,2048,128]{3,2,1,0:T(8,128)S(1)} %pad_maximum_fusion.9) | data formatting | bytes 4194304 | tf_op jit(solution)/shard_map/while/body/eval_jaxpr/stack | solution.py:127
  145.9 31.4 %all-to-all-done.2 = f32[2,1,2048,128]{3,1,0,2:T(1,128)} async-done(((f32[2,1,2048,128]{3,1,0,2:T(1,128)}), f32[2,1,2048,128]{3,1,0,2:T(1,128)}, u32[]{:S(2)}, u32[]{:S(2)}) %all-to-all-start.2) | async-done | bytes 2097184 | tf_op jit(solution)/shard_map/while/body/eval_jaxpr/all_to_all | solution.py:130
  202.3 27.2 %all-to-all-done.1 = f32[2,1,2048,128]{3,1,0,2:T(1,128)S(1)} async-done(((f32[2,1,2048,128]{3,1,0,2:T(1,128)}), f32[2,1,2048,128]{3,1,0,2:T(1,128)S(1)}, u32[]{:S(2)}, u32[]{:S(2)}) %all-to-all-start.1) | async-done | bytes 2097184 | tf_op jit(solution)/shard_map/while/body/eval_jaxpr/all_to_all | solution.py:130
  255.7 10.9 %fusion.706 = (f32[1,1,128,2048]{3,2,1,0:T(8,128)S(1)}, f32[1,1,128,2048]{3,2,1,0:T(8,128)S(1)}) fusion(f32[16,8,16,128]{3,2,1,0:T(8,128)} %bitcast.711, f32[16,8,16,128]{3,2,1,0:T(8,128)S(1)} %bitcast.710, f32[16,8,16,128]{3,2,1,0:T(8,128)S(1)} %bitcast.709, f32[16,8,16,128]{3,2,1,0:T(8,128)S(1)} %bitcast.708, f32[]{:T(128)} %bitcast.679, ...), kind=kLoop, calls=%fused_computation.70.clone.1 | loop fusion | flops 6815744 | bytes 7340048 | tf_op jit(solution)/shard_map/while/body/eval_jaxpr/stack | solution.py:144
  290.1 10.2 %fusion.669 = (f32[2048,128]{1,0:T(8,128)}, f32[2048,128]{1,0:T(8,128)}, f32[2048,128]{1,0:T(8,128)S(1)}, f32[2048,128]{1,0:T(8,128)}) fusion(f32[128]{0:T(128)S(1)} %get-tuple-element.413, f32[2048]{0:T(1024)S(1)} %get-tuple-element.414, f32[]{:T(128)} %bitcast.650, f32[]{:T(128)} %bitcast.652), kind=kLoop, calls=%fused_computation.62.clone.1 | loop fusion | flops 3932160 | bytes 4203016 | tf_op jit(solution)/shard_map/while/body/eval_jaxpr/jit(_where)/select_n | solution.py:123
  309.3 24.8 %all-to-all-done = f32[2,1,128,2048]{2,1,0,3:T(1,128)S(1)} async-done(((f32[2,1,128,2048]{2,1,0,3:T(1,128)}), f32[2,1,128,2048]{2,1,0,3:T(1,128)S(1)}, u32[]{:S(2)}, u32[]{:S(2)}) %all-to-all-start) | async-done | bytes 2097184 | tf_op jit(solution)/shard_map/while/body/eval_jaxpr/all_to_all | solution.py:111
  371.8 10.2 %copy.403 = f32[2,1,2048,128]{3,1,0,2:T(1,128)} copy(f32[2,1,2048,128]{3,2,1,0:T(8,128)S(1)} %pad_maximum_fusion.10) | data formatting | bytes 4194304 | tf_op jit(solution)/shard_map/while/body/eval_jaxpr/stack | solution.py:127
  393.0 10.0 %copy.396 = f32[2,1,2048,128]{3,1,0,2:T(1,128)} copy(f32[2,1,2048,128]{3,2,1,0:T(8,128)S(1)} %pad_maximum_fusion.9) | data formatting | bytes 4194304 | tf_op jit(solution)/shard_map/while/body/eval_jaxpr/stack | solution.py:127
  403.0 31.4 %all-to-all-done.2 = f32[2,1,2048,128]{3,1,0,2:T(1,128)} async-done(((f32[2,1,2048,128]{3,1,0,2:T(1,128)}), f32[2,1,2048,128]{3,1,0,2:T(1,128)}, u32[]{:S(2)}, u32[]{:S(2)}) %all-to-all-start.2) | async-done | bytes 2097184 | tf_op jit(solution)/shard_map/while/body/eval_jaxpr/all_to_all | solution.py:130
  459.2 27.4 %all-to-all-done.1 = f32[2,1,2048,128]{3,1,0,2:T(1,128)S(1)} async-done(((f32[2,1,2048,128]{3,1,0,2:T(1,128)}), f32[2,1,2048,128]{3,1,0,2:T(1,128)S(1)}, u32[]{:S(2)}, u32[]{:S(2)}) %all-to-all-start.1) | async-done | bytes 2097184 | tf_op jit(solution)/shard_map/while/body/eval_jaxpr/all_to_all | solution.py:130
  513.0 10.9 %fusion.706 = (f32[1,1,128,2048]{3,2,1,0:T(8,128)S(1)}, f32[1,1,128,2048]{3,2,1,0:T(8,128)S(1)}) fusion(f32[16,8,16,128]{3,2,1,0:T(8,128)} %bitcast.711, f32[16,8,16,128]{3,2,1,0:T(8,128)S(1)} %bitcast.710, f32[16,8,16,128]{3,2,1,0:T(8,128)S(1)} %bitcast.709, f32[16,8,16,128]{3,2,1,0:T(8,128)S(1)} %bitcast.708, f32[]{:T(128)} %bitcast.679, ...), kind=kLoop, calls=%fused_computation.70.clone.1 | loop fusion | flops 6815744 | bytes 7340048 | tf_op jit(solution)/shard_map/while/body/eval_jaxpr/stack | solution.py:144
  547.4 10.2 %fusion.669 = (f32[2048,128]{1,0:T(8,128)}, f32[2048,128]{1,0:T(8,128)}, f32[2048,128]{1,0:T(8,128)S(1)}, f32[2048,128]{1,0:T(8,128)}) fusion(f32[128]{0:T(128)S(1)} %get-tuple-element.413, f32[2048]{0:T(1024)S(1)} %get-tuple-element.414, f32[]{:T(128)} %bitcast.650, f32[]{:T(128)} %bitcast.652), kind=kLoop, calls=%fused_computation.62.clone.1 | loop fusion | flops 3932160 | bytes 4203016 | tf_op jit(solution)/shard_map/while/body/eval_jaxpr/jit(_where)/select_n | solution.py:123
  566.6 24.8 %all-to-all-done = f32[2,1,128,2048]{2,1,0,3:T(1,128)S(1)} async-done(((f32[2,1,128,2048]{2,1,0,3:T(1,128)}), f32[2,1,128,2048]{2,1,0,3:T(1,128)S(1)}, u32[]{:S(2)}, u32[]{:S(2)}) %all-to-all-start) | async-done | bytes 2097184 | tf_op jit(solution)/shard_map/while/body/eval_jaxpr/all_to_all | solution.py:111
  628.9 10.4 %copy.403 = f32[2,1,2048,128]{3,1,0,2:T(1,128)} copy(f32[2,1,2048,128]{3,2,1,0:T(8,128)S(1)} %pad_maximum_fusion.10) | data formatting | bytes 4194304 | tf_op jit(solution)/shard_map/while/body/eval_jaxpr/stack | solution.py:127
  639.3 4.9 all-to-all-start.2
  650.3 10.0 %copy.396 = f32[2,1,2048,128]{3,1,0,2:T(1,128)} copy(f32[2,1,2048,128]{3,2,1,0:T(8,128)S(1)} %pad_maximum_fusion.9) | data formatting | bytes 4194304 | tf_op jit(solution)/shard_map/while/body/eval_jaxpr/stack | solution.py:127
  660.3 31.4 %all-to-all-done.2 = f32[2,1,2048,128]{3,1,0,2:T(1,128)} async-done(((f32[2,1,2048,128]{3,1,0,2:T(1,128)}), f32[2,1,2048,128]{3,1,0,2:T(1,128)}, u32[]{:S(2)}, u32[]{:S(2)}) %all-to-all-start.2) | async-done | bytes 2097184 | tf_op jit(solution)/shard_map/while/body/eval_jaxpr/all_to_all | solution.py:130
  716.4 27.5 %all-to-all-done.1 = f32[2,1,2048,128]{3,1,0,2:T(1,128)S(1)} async-done(((f32[2,1,2048,128]{3,1,0,2:T(1,128)}), f32[2,1,2048,128]{3,1,0,2:T(1,128)S(1)}, u32[]{:S(2)}, u32[]{:S(2)}) %all-to-all-start.1) | async-done | bytes 2097184 | tf_op jit(solution)/shard_map/while/body/eval_jaxpr/all_to_all | solution.py:130
  770.3 10.9 %fusion.706 = (f32[1,1,128,2048]{3,2,1,0:T(8,128)S(1)}, f32[1,1,128,2048]{3,2,1,0:T(8,128)S(1)}) fusion(f32[16,8,16,128]{3,2,1,0:T(8,128)} %bitcast.711, f32[16,8,16,128]{3,2,1,0:T(8,128)S(1)} %bitcast.710, f32[16,8,16,128]{3,2,1,0:T(8,128)S(1)} %bitcast.709, f32[16,8,16,128]{3,2,1,0:T(8,128)S(1)} %bitcast.708, f32[]{:T(128)} %bitcast.679, ...), kind=kLoop, calls=%fused_computation.70.clone.1 | loop fusion | flops 6815744 | bytes 7340048 | tf_op jit(solution)/shard_map/while/body/eval_jaxpr/stack | solution.py:144
  (324 shorter events, 375.6 us)
Async XLA Ops:
  23.0 53.9 %all-to-all-start = ((f32[2,1,128,2048]{2,1,0,3:T(1,128)}), f32[2,1,128,2048]{2,1,0,3:T(1,128)S(1)}, u32[]{:S(2)}, u32[]{:S(2)}) async-start(f32[2,1,128,2048]{2,1,0,3:T(1,128)} %pad_maximum_fusion.8), calls=%async_computation | async-start | bytes 4194304 | tf_op jit(solution)/shard_map/while/body/eval_jaxpr/all_to_all | solution.py:111
  89.8 2.5 copy-start.7
  91.1 1.8 copy-start.6
  124.9 4.9 copy-start.2
  124.9 52.4 %all-to-all-start.2 = ((f32[2,1,2048,128]{3,1,0,2:T(1,128)}), f32[2,1,2048,128]{3,1,0,2:T(1,128)}, u32[]{:S(2)}, u32[]{:S(2)}) async-start(f32[2,1,2048,128]{3,1,0,2:T(1,128)} %copy.403), calls=%async_computation.2 | async-start | bytes 4194304 | tf_op jit(solution)/shard_map/while/body/eval_jaxpr/all_to_all | solution.py:130
  177.3 52.2 %all-to-all-start.1 = ((f32[2,1,2048,128]{3,1,0,2:T(1,128)}), f32[2,1,2048,128]{3,1,0,2:T(1,128)S(1)}, u32[]{:S(2)}, u32[]{:S(2)}) async-start(f32[2,1,2048,128]{3,1,0,2:T(1,128)} %copy.396), calls=%async_computation.1 | async-start | bytes 4194304 | tf_op jit(solution)/shard_map/while/body/eval_jaxpr/all_to_all | solution.py:130
  182.1 73.6 %all-gather.6.cloned.1.call-start = ((), (), s32[]{:S(2)}) async-start(), calls=%async_computation.3 | async-start | bytes 1572864 | tf_op jit(solution)/shard_map/while/body/eval_jaxpr/all_gather | solution.py:108
  235.2 3.9 copy-start.1
  282.0 52.2 %all-to-all-start = ((f32[2,1,128,2048]{2,1,0,3:T(1,128)}), f32[2,1,128,2048]{2,1,0,3:T(1,128)S(1)}, u32[]{:S(2)}, u32[]{:S(2)}) async-start(f32[2,1,128,2048]{2,1,0,3:T(1,128)} %pad_maximum_fusion.8), calls=%async_computation | async-start | bytes 4194304 | tf_op jit(solution)/shard_map/while/body/eval_jaxpr/all_to_all | solution.py:111
  346.7 2.5 copy-start.7
  348.0 1.8 copy-start.6
  382.0 4.9 copy-start.2
  382.0 52.4 %all-to-all-start.2 = ((f32[2,1,2048,128]{3,1,0,2:T(1,128)}), f32[2,1,2048,128]{3,1,0,2:T(1,128)}, u32[]{:S(2)}, u32[]{:S(2)}) async-start(f32[2,1,2048,128]{3,1,0,2:T(1,128)} %copy.403), calls=%async_computation.2 | async-start | bytes 4194304 | tf_op jit(solution)/shard_map/while/body/eval_jaxpr/all_to_all | solution.py:130
  434.4 52.2 %all-to-all-start.1 = ((f32[2,1,2048,128]{3,1,0,2:T(1,128)}), f32[2,1,2048,128]{3,1,0,2:T(1,128)S(1)}, u32[]{:S(2)}, u32[]{:S(2)}) async-start(f32[2,1,2048,128]{3,1,0,2:T(1,128)} %copy.396), calls=%async_computation.1 | async-start | bytes 4194304 | tf_op jit(solution)/shard_map/while/body/eval_jaxpr/all_to_all | solution.py:130
  439.2 73.8 %all-gather.6.cloned.1.call-start = ((), (), s32[]{:S(2)}) async-start(), calls=%async_computation.3 | async-start | bytes 1572864 | tf_op jit(solution)/shard_map/while/body/eval_jaxpr/all_gather | solution.py:108
  492.5 3.9 copy-start.1
  539.3 52.2 %all-to-all-start = ((f32[2,1,128,2048]{2,1,0,3:T(1,128)}), f32[2,1,128,2048]{2,1,0,3:T(1,128)S(1)}, u32[]{:S(2)}, u32[]{:S(2)}) async-start(f32[2,1,128,2048]{2,1,0,3:T(1,128)} %pad_maximum_fusion.8), calls=%async_computation | async-start | bytes 4194304 | tf_op jit(solution)/shard_map/while/body/eval_jaxpr/all_to_all | solution.py:111
  603.9 2.5 copy-start.7
  605.2 1.8 copy-start.6
  639.3 4.9 copy-start.2
  639.3 52.4 %all-to-all-start.2 = ((f32[2,1,2048,128]{3,1,0,2:T(1,128)}), f32[2,1,2048,128]{3,1,0,2:T(1,128)}, u32[]{:S(2)}, u32[]{:S(2)}) async-start(f32[2,1,2048,128]{3,1,0,2:T(1,128)} %copy.403), calls=%async_computation.2 | async-start | bytes 4194304 | tf_op jit(solution)/shard_map/while/body/eval_jaxpr/all_to_all | solution.py:130
  691.7 52.2 %all-to-all-start.1 = ((f32[2,1,2048,128]{3,1,0,2:T(1,128)}), f32[2,1,2048,128]{3,1,0,2:T(1,128)S(1)}, u32[]{:S(2)}, u32[]{:S(2)}) async-start(f32[2,1,2048,128]{3,1,0,2:T(1,128)} %copy.396), calls=%async_computation.1 | async-start | bytes 4194304 | tf_op jit(solution)/shard_map/while/body/eval_jaxpr/all_to_all | solution.py:130
  696.5 73.8 %all-gather.6.cloned.1.call-start = ((), (), s32[]{:S(2)}) async-start(), calls=%async_computation.3 | async-start | bytes 1572864 | tf_op jit(solution)/shard_map/while/body/eval_jaxpr/all_gather | solution.py:108
  749.6 3.9 copy-start.1
  (15 other events, 20.7 us)
Sparse Core Ops, SparseCore 0:
  184.5 21.7 all-gather.5
  441.5 21.7 all-gather.5
  698.8 21.7 all-gather.5
where the time goes:
time: 794 us; the launch traced here: 791 us
  waiting for transfers between devices  251 us (32%)
  matrix products  223 us (28%)
  local copies, waits for them, and re-layouts  167 us (21%)
  other arithmetic  75.2 us (9%)
  starting transfers between devices  45.2 us (6%)
  loops' own time  14.6 us (2%)
  between operations  14.1 us (2%)
    dot_general x144, matrix products, product(): return jnp.einsum(form, matrix, data, precision=lax.Precision.HIGHEST)  223 us
    all_to_all x6, waiting for transfers between devices, advance(): lax.all_to_all(shifted[branch], 'slab', split_axis=2, concat_axis=3, tile...  176 us
    all_to_all x3, waiting for transfers between devices, advance(): lax.all_to_all(jnp.stack((real, imag)), 'slab', split_axis=3, concat_axis...  74.5 us
    another operation x6, local copies, waits for them, and re-layouts, advance(): shifted.append(jnp.stack((back_real, back_imag)))  60.7 us
    another operation x6, other arithmetic, advance(): return jnp.stack((new_real, new_imag))  33.4 us
    select_n x3, other arithmetic, advance(): prop_imag = jnp.where(live, jnp.sin(angle), jnp.zeros_like(angle))  30.7 us
    all_to_all x12, local copies, waits for them, and re-layouts, advance(): lax.all_to_all(shifted[branch], 'slab', split_axis=2, concat_axis=3, tile...  29.5 us
    all_to_all x6, starting transfers between devices, advance(): lax.all_to_all(shifted[branch], 'slab', split_axis=2, concat_axis=3, tile...  29 us
  transfers between devices with their start and end apart: 12, of which 9 were waited for; matrix products, arithmetic and copies ran while one was open for 31% of the time, Pallas kernels for 0%

commit v1 on v0

--- a/solution.py
+++ b/solution.py
@@ -6,6 +6,29 @@
 
 two_pi = 2.0 * math.pi
 depth_step = 2.0
+
+
+def in_blocks(x, dim, size):
+    dims = x.shape
+    blocks = x.reshape(*dims[:dim], size, dims[dim] // size, *dims[dim + 1 :])
+    return jnp.moveaxis(blocks, dim, 0)
+
+
+def joined_along(pieces, dim):
+    lengths = list(pieces.shape[1:])
+    lengths[dim] *= pieces.shape[0]
+    return jnp.moveaxis(pieces, 0, dim).reshape(lengths)
+
+
+def rotated_exchange(x, axis, split_dim, concat_dim):
+    size, index = (lax.axis_size(axis), lax.axis_index(axis))
+    blocks = in_blocks(x, split_dim, size)
+    finished = [blocks[index]]
+    for step in range(1, size):
+        sent = blocks[(index + step) % size]
+        finished.append(lax.ppermute(sent, axis, [(i, (i + step) % size) for i in range(size)]))
+    blocks = jnp.stack(finished)[(index - jnp.arange(size)) % size]
+    return joined_along(blocks, concat_dim)
 
 
 def dft_matrix(length, sign):
@@ -107,9 +130,7 @@
         local_tile = lax.dynamic_index_in_dim(velocity, level, 0, keepdims=False)
         tile = lax.all_gather(local_tile, "freq", axis=1, tiled=True)
         real, imag = transform(field[0], field[1], False, -1)
-        spectrum = forward_x(
-            lax.all_to_all(jnp.stack((real, imag)), "slab", split_axis=3, concat_axis=2, tiled=True)
-        )
+        spectrum = forward_x(rotated_exchange(jnp.stack((real, imag)), "slab", 3, 2))
         slow_pair = lax.dynamic_index_in_dim(ref_slow, level, 0, keepdims=False)
         slowness = 1.0 / tile
         upper_weight = jnp.clip((slowness - slow_pair[0]) / (slow_pair[1] - slow_pair[0]), 0.0, 1.0)

time: 794 us -> 866 us (1.091)
  starting transfers between devices: 45.2 us -> 104 us
  local copies, waits for them, and re-layouts: 167 us -> 188 us
    all_to_all x3 -> x0, waiting for transfers between devices: 74.5 us -> none  [advance(): lax.all_to_all(jnp.stack((real, imag)), 'slab', split_axis=3, concat_axis...]
    ppermute x0 -> x45, waiting for transfers between devices: none -> 67.1 us  [rotated_exchange(): lax.ppermute(sent, axis, [(i, (i + step) % size) for i in range(size)])]
    ppermute x0 -> x45, starting transfers between devices: none -> 62.9 us  [rotated_exchange(): lax.ppermute(sent, axis, [(i, (i + step) % size) for i in range(size)])]
    all_to_all x3 -> x0, starting transfers between devices: 16.1 us -> none  [advance(): lax.all_to_all(jnp.stack((real, imag)), 'slab', split_axis=3, concat_axis...]
    while x60 -> x168, local copies, waits for them, and re-layouts: 8.15 us -> 21.9 us
    all_to_all x6, starting transfers between devices: 29 us -> 40.9 us  [advance(): lax.all_to_all(shifted[branch], 'slab', split_axis=2, concat_axis=3, tile...]
    gather x0 -> x6, local copies, waits for them, and re-layouts: none -> 10.8 us  [rotated_exchange(): blocks = jnp.stack(finished)[(index - jnp.arange(size)) % size]]
    another operation x3 -> x0, other arithmetic: 9.91 us -> none  [advance(): jnp.stack((real, imag))]
  transfers between devices with their start and end apart: 12 -> 54, of which waited for: 9 -> 23; matrix products, arithmetic and copies ran while one was open for 31% -> 31% of each run, Pallas kernels for 0% -> 0%
where the time goes in v1:
time: 866 us; the launch traced here: 862 us
  waiting for transfers between devices  243 us (28%)
  matrix products  222 us (26%)
  local copies, waits for them, and re-layouts  188 us (22%)
  starting transfers between devices  104 us (12%)
  other arithmetic  74.8 us (9%)
  loops' own time  16.3 us (2%)
  between operations  14.1 us (2%)
    dot_general x144, matrix products, product(): return jnp.einsum(form, matrix, data, precision=lax.Precision.HIGHEST)  222 us
    all_to_all x6, waiting for transfers between devices, advance(): lax.all_to_all(shifted[branch], 'slab', split_axis=2, concat_axis=3, tile...  176 us
    ppermute x45, waiting for transfers between devices, rotated_exchange(): lax.ppermute(sent, axis, [(i, (i + step) % size) for i in range(size)])  67.1 us
    ppermute x45, starting transfers between devices, rotated_exchange(): lax.ppermute(sent, axis, [(i, (i + step) % size) for i in range(size)])  62.9 us
    another operation x6, local copies, waits for them, and re-layouts, advance(): shifted.append(jnp.stack((back_real, back_imag)))  60.7 us
    all_to_all x6, starting transfers between devices, advance(): lax.all_to_all(shifted[branch], 'slab', split_axis=2, concat_axis=3, tile...  40.9 us
    another operation x6, other arithmetic, advance(): return jnp.stack((new_real, new_imag))  33.6 us
    select_n x3, other arithmetic, advance(): prop_imag = jnp.where(live, jnp.sin(angle), jnp.zeros_like(angle))  30.8 us
  transfers between devices with their start and end apart: 54, of which 23 were waited for; matrix products, arithmetic and copies ran while one was open for 31% of the time, Pallas kernels for 0%

profile of v1, /device:TPU:11, one launch (start us, length us, event | category | flops | bytes accessed | tf_op | source)
XLA Modules:
  0.0 861.8 jit_solution(411018378671379160)
XLA Ops:
  8.1 845.6 %while.17 = (s32[]{:T(128)}, f32[2,1,128,2048]{3,2,1,0:T(8,128)S(1)}, f32[3,128,1024]{2,1,0:T(8,128)}, f32[3,2]{0,1:T(2,128)S(1)}, f32[1,1,1]{2,1,0:T(1,128)}, /...) while((s32[]{:T(128)}, ...), condition=%wide.region_1.2_spmd.clone, body=%wide.region_0.1_spmd.clone.sunk | while | flops 10909408256 | bytes 344036064 | solution.py:167
  31.1 10.3 %fusion.710 = (f32[2048,128]{1,0:T(8,128)}, f32[2048,128]{1,0:T(8,128)}, f32[2048,128]{1,0:T(8,128)S(1)}, f32[2048,128]{1,0:T(8,128)}) fusion(f32[128]{0:T(128)S(1)} %get-tuple-element.492, f32[2048]{0:T(1024)S(1)} %get-tuple-element.493, f32[]{:T(128)} %bitcast.754, f32[]{:T(128)} %bitcast.756), kind=kLoop, calls=%fused_computation.97.clone.1 | loop fusion | flops 3932160 | bytes 4203016 | tf_op jit(solution)/shard_map/while/body/eval_jaxpr/jit(_where)/select_n | solution.py:144
  62.6 9.7 %collective-permute-done.4 = f32[2,1,128,128]{3,2,0,1:T(8,128)S(1)} collective-permute-done((f32[2,1,128,128]{3,2,0,1:T(8,128)}, f32[2,1,128,128]{3,2,0,1:T(8,128)S(1)}, u32[]{:S(2)}, u32[]{:S(2)}) %collective-permute-start.4) | collective-permute-done | bytes 131104 | tf_op jit(solution)/shard_map/while/body/eval_jaxpr/ppermute | solution.py:29
  134.0 10.2 %copy.369 = f32[2,1,2048,128]{3,1,0,2:T(1,128)} copy(f32[2,1,2048,128]{3,2,1,0:T(8,128)S(1)} %pad_maximum_fusion.7) | data formatting | bytes 4194304 | tf_op jit(solution)/shard_map/while/body/eval_jaxpr/stack | solution.py:148
  156.9 10.0 %copy.362 = f32[2,1,2048,128]{3,1,0,2:T(1,128)} copy(f32[2,1,2048,128]{3,2,1,0:T(8,128)S(1)} %pad_maximum_fusion.6) | data formatting | bytes 4194304 | tf_op jit(solution)/shard_map/while/body/eval_jaxpr/stack | solution.py:148
  166.9 31.4 %all-to-all-done.1 = f32[2,1,2048,128]{3,1,0,2:T(1,128)} async-done(((f32[2,1,2048,128]{3,1,0,2:T(1,128)}), f32[2,1,2048,128]{3,1,0,2:T(1,128)}, u32[]{:S(2)}, u32[]{:S(2)}) %all-to-all-start.1) | async-done | bytes 2097184 | tf_op jit(solution)/shard_map/while/body/eval_jaxpr/all_to_all | solution.py:151
  223.5 27.0 %all-to-all-done = f32[2,1,2048,128]{3,1,0,2:T(1,128)S(1)} async-done(((f32[2,1,2048,128]{3,1,0,2:T(1,128)}), f32[2,1,2048,128]{3,1,0,2:T(1,128)S(1)}, u32[]{:S(2)}, u32[]{:S(2)}) %all-to-all-start) | async-done | bytes 2097184 | tf_op jit(solution)/shard_map/while/body/eval_jaxpr/all_to_all | solution.py:151
  276.7 11.0 %fusion.753 = (f32[1,1,128,2048]{3,2,1,0:T(8,128)S(1)}, f32[1,1,128,2048]{3,2,1,0:T(8,128)S(1)}) fusion(f32[16,8,16,128]{3,2,1,0:T(8,128)} %bitcast.812, f32[16,8,16,128]{3,2,1,0:T(8,128)S(1)} %bitcast.811, f32[16,8,16,128]{3,2,1,0:T(8,128)S(1)} %bitcast.810, f32[16,8,16,128]{3,2,1,0:T(8,128)S(1)} %bitcast.809, f32[]{:T(128)} %bitcast.781, ...), kind=kLoop, calls=%fused_computation.105.clone.1 | loop fusion | flops 6815744 | bytes 7340048 | tf_op jit(solution)/shard_map/while/body/eval_jaxpr/stack | solution.py:165
  311.2 10.3 %fusion.710 = (f32[2048,128]{1,0:T(8,128)}, f32[2048,128]{1,0:T(8,128)}, f32[2048,128]{1,0:T(8,128)S(1)}, f32[2048,128]{1,0:T(8,128)}) fusion(f32[128]{0:T(128)S(1)} %get-tuple-element.492, f32[2048]{0:T(1024)S(1)} %get-tuple-element.493, f32[]{:T(128)} %bitcast.754, f32[]{:T(128)} %bitcast.756), kind=kLoop, calls=%fused_computation.97.clone.1 | loop fusion | flops 3932160 | bytes 4203016 | tf_op jit(solution)/shard_map/while/body/eval_jaxpr/jit(_where)/select_n | solution.py:144
  341.9 10.2 %collective-permute-done.4 = f32[2,1,128,128]{3,2,0,1:T(8,128)S(1)} collective-permute-done((f32[2,1,128,128]{3,2,0,1:T(8,128)}, f32[2,1,128,128]{3,2,0,1:T(8,128)S(1)}, u32[]{:S(2)}, u32[]{:S(2)}) %collective-permute-start.4) | collective-permute-done | bytes 131104 | tf_op jit(solution)/shard_map/while/body/eval_jaxpr/ppermute | solution.py:29
  412.6 10.2 %copy.369 = f32[2,1,2048,128]{3,1,0,2:T(1,128)} copy(f32[2,1,2048,128]{3,2,1,0:T(8,128)S(1)} %pad_maximum_fusion.7) | data formatting | bytes 4194304 | tf_op jit(solution)/shard_map/while/body/eval_jaxpr/stack | solution.py:148
  422.7 10.0 %all-to-all-start.1 = ((f32[2,1,2048,128]{3,1,0,2:T(1,128)}), f32[2,1,2048,128]{3,1,0,2:T(1,128)}, u32[]{:S(2)}, u32[]{:S(2)}) async-start(f32[2,1,2048,128]{3,1,0,2:T(1,128)} %copy.369), calls=%async_computation.1 | async-start | bytes 4194304 | tf_op jit(solution)/shard_map/while/body/eval_jaxpr/all_to_all | solution.py:151
  438.9 10.0 %copy.362 = f32[2,1,2048,128]{3,1,0,2:T(1,128)} copy(f32[2,1,2048,128]{3,2,1,0:T(8,128)S(1)} %pad_maximum_fusion.6) | data formatting | bytes 4194304 | tf_op jit(solution)/shard_map/while/body/eval_jaxpr/stack | solution.py:148
  448.8 31.4 %all-to-all-done.1 = f32[2,1,2048,128]{3,1,0,2:T(1,128)} async-done(((f32[2,1,2048,128]{3,1,0,2:T(1,128)}), f32[2,1,2048,128]{3,1,0,2:T(1,128)}, u32[]{:S(2)}, u32[]{:S(2)}) %all-to-all-start.1) | async-done | bytes 2097184 | tf_op jit(solution)/shard_map/while/body/eval_jaxpr/all_to_all | solution.py:151
  505.2 27.2 %all-to-all-done = f32[2,1,2048,128]{3,1,0,2:T(1,128)S(1)} async-done(((f32[2,1,2048,128]{3,1,0,2:T(1,128)}), f32[2,1,2048,128]{3,1,0,2:T(1,128)S(1)}, u32[]{:S(2)}, u32[]{:S(2)}) %all-to-all-start) | async-done | bytes 2097184 | tf_op jit(solution)/shard_map/while/body/eval_jaxpr/all_to_all | solution.py:151
  558.8 11.0 %fusion.753 = (f32[1,1,128,2048]{3,2,1,0:T(8,128)S(1)}, f32[1,1,128,2048]{3,2,1,0:T(8,128)S(1)}) fusion(f32[16,8,16,128]{3,2,1,0:T(8,128)} %bitcast.812, f32[16,8,16,128]{3,2,1,0:T(8,128)S(1)} %bitcast.811, f32[16,8,16,128]{3,2,1,0:T(8,128)S(1)} %bitcast.810, f32[16,8,16,128]{3,2,1,0:T(8,128)S(1)} %bitcast.809, f32[]{:T(128)} %bitcast.781, ...), kind=kLoop, calls=%fused_computation.105.clone.1 | loop fusion | flops 6815744 | bytes 7340048 | tf_op jit(solution)/shard_map/while/body/eval_jaxpr/stack | solution.py:165
  593.3 10.3 %fusion.710 = (f32[2048,128]{1,0:T(8,128)}, f32[2048,128]{1,0:T(8,128)}, f32[2048,128]{1,0:T(8,128)S(1)}, f32[2048,128]{1,0:T(8,128)}) fusion(f32[128]{0:T(128)S(1)} %get-tuple-element.492, f32[2048]{0:T(1024)S(1)} %get-tuple-element.493, f32[]{:T(128)} %bitcast.754, f32[]{:T(128)} %bitcast.756), kind=kLoop, calls=%fused_computation.97.clone.1 | loop fusion | flops 3932160 | bytes 4203016 | tf_op jit(solution)/shard_map/while/body/eval_jaxpr/jit(_where)/select_n | solution.py:144
  624.1 10.2 %collective-permute-done.4 = f32[2,1,128,128]{3,2,0,1:T(8,128)S(1)} collective-permute-done((f32[2,1,128,128]{3,2,0,1:T(8,128)}, f32[2,1,128,128]{3,2,0,1:T(8,128)S(1)}, u32[]{:S(2)}, u32[]{:S(2)}) %collective-permute-start.4) | collective-permute-done | bytes 131104 | tf_op jit(solution)/shard_map/while/body/eval_jaxpr/ppermute | solution.py:29
  694.5 10.4 %copy.369 = f32[2,1,2048,128]{3,1,0,2:T(1,128)} copy(f32[2,1,2048,128]{3,2,1,0:T(8,128)S(1)} %pad_maximum_fusion.7) | data formatting | bytes 4194304 | tf_op jit(solution)/shard_map/while/body/eval_jaxpr/stack | solution.py:148
  704.9 10.0 %all-to-all-start.1 = ((f32[2,1,2048,128]{3,1,0,2:T(1,128)}), f32[2,1,2048,128]{3,1,0,2:T(1,128)}, u32[]{:S(2)}, u32[]{:S(2)}) async-start(f32[2,1,2048,128]{3,1,0,2:T(1,128)} %copy.369), calls=%async_computation.1 | async-start | bytes 4194304 | tf_op jit(solution)/shard_map/while/body/eval_jaxpr/all_to_all | solution.py:151
  721.0 10.0 %copy.362 = f32[2,1,2048,128]{3,1,0,2:T(1,128)} copy(f32[2,1,2048,128]{3,2,1,0:T(8,128)S(1)} %pad_maximum_fusion.6) | data formatting | bytes 4194304 | tf_op jit(solution)/shard_map/while/body/eval_jaxpr/stack | solution.py:148
  731.0 31.4 %all-to-all-done.1 = f32[2,1,2048,128]{3,1,0,2:T(1,128)} async-done(((f32[2,1,2048,128]{3,1,0,2:T(1,128)}), f32[2,1,2048,128]{3,1,0,2:T(1,128)}, u32[]{:S(2)}, u32[]{:S(2)}) %all-to-all-start.1) | async-done | bytes 2097184 | tf_op jit(solution)/shard_map/while/body/eval_jaxpr/all_to_all | solution.py:151
  787.3 27.3 %all-to-all-done = f32[2,1,2048,128]{3,1,0,2:T(1,128)S(1)} async-done(((f32[2,1,2048,128]{3,1,0,2:T(1,128)}), f32[2,1,2048,128]{3,1,0,2:T(1,128)S(1)}, u32[]{:S(2)}, u32[]{:S(2)}) %all-to-all-start) | async-done | bytes 2097184 | tf_op jit(solution)/shard_map/while/body/eval_jaxpr/all_to_all | solution.py:151
  841.0 11.0 %fusion.753 = (f32[1,1,128,2048]{3,2,1,0:T(8,128)S(1)}, f32[1,1,128,2048]{3,2,1,0:T(8,128)S(1)}) fusion(f32[16,8,16,128]{3,2,1,0:T(8,128)} %bitcast.812, f32[16,8,16,128]{3,2,1,0:T(8,128)S(1)} %bitcast.811, f32[16,8,16,128]{3,2,1,0:T(8,128)S(1)} %bitcast.810, f32[16,8,16,128]{3,2,1,0:T(8,128)S(1)} %bitcast.809, f32[]{:T(128)} %bitcast.781, ...), kind=kLoop, calls=%fused_computation.105.clone.1 | loop fusion | flops 6815744 | bytes 7340048 | tf_op jit(solution)/shard_map/while/body/eval_jaxpr/stack | solution.py:165
  (537 shorter events, 481.1 us)
Async XLA Ops:
  20.0 52.4 %collective-permute-start.5 = (f32[2,1,128,128]{3,2,0,1:T(8,128)}, f32[2,1,128,128]{3,2,0,1:T(8,128)}, u32[]{:S(2)}, u32[]{:S(2)}) collective-permute-start(f32[2,1,128,128]{3,2,0,1:T(8,128)} %get-tuple-element.399), channel_id=1, source_target_pairs={{0,6},{1,7},{2,8},{3,9},{4,10},{5,11},{6,12},{7,13},{8,14},{9,15},... | collective-permute-start | bytes 393224 | tf_op jit(solution)/shard_map/while/body/eval_jaxpr/ppermute | solution.py:29
  23.1 28.7 %collective-permute-start = (f32[2,1,128,128]{3,2,0,1:T(8,128)}, f32[2,1,128,128]{3,2,0,1:T(8,128)}, u32[]{:S(2)}, u32[]{:S(2)}) collective-permute-start(f32[2,1,128,128]{3,2,0,1:T(8,128)} %get-tuple-element.394), channel_id=1, source_target_pairs={{0,1},{1,2},{2,3},{3,4},{4,5},{5,6},{6,7},{7,8},{8,9},{9,10},{10,1... | collective-permute-start | bytes 393224 | tf_op jit(solution)/shard_map/while/body/eval_jaxpr/ppermute | solution.py:29
  25.2 31.4 %collective-permute-start.1 = (f32[2,1,128,128]{3,2,0,1:T(8,128)}, f32[2,1,128,128]{3,2,0,1:T(8,128)}, u32[]{:S(2)}, u32[]{:S(2)}) collective-permute-start(f32[2,1,128,128]{3,2,0,1:T(8,128)} %get-tuple-element.395), channel_id=1, source_target_pairs={{0,2},{1,3},{2,4},{3,5},{4,6},{5,7},{6,8},{7,9},{8,10},{9,11},{10,... | collective-permute-start | bytes 393224 | tf_op jit(solution)/shard_map/while/body/eval_jaxpr/ppermute | solution.py:29
  25.2 33.9 %collective-permute-start.2 = (f32[2,1,128,128]{3,2,0,1:T(8,128)}, f32[2,1,128,128]{3,2,0,1:T(8,128)}, u32[]{:S(2)}, u32[]{:S(2)}) collective-permute-start(f32[2,1,128,128]{3,2,0,1:T(8,128)} %get-tuple-element.396), channel_id=1, source_target_pairs={{0,3},{1,4},{2,5},{3,6},{4,7},{5,8},{6,9},{7,10},{8,11},{9,12},{10... | collective-permute-start | bytes 393224 | tf_op jit(solution)/shard_map/while/body/eval_jaxpr/ppermute | solution.py:29
  25.4 34.8 %collective-permute-start.3 = (f32[2,1,128,128]{3,2,0,1:T(8,128)}, f32[2,1,128,128]{3,2,0,1:T(8,128)}, u32[]{:S(2)}, u32[]{:S(2)}) collective-permute-start(f32[2,1,128,128]{3,2,0,1:T(8,128)} %get-tuple-element.397), channel_id=1, source_target_pairs={{0,4},{1,5},{2,6},{3,7},{4,8},{5,9},{6,10},{7,11},{8,12},{9,13},{1... | collective-permute-start | bytes 393224 | tf_op jit(solution)/shard_map/while/body/eval_jaxpr/ppermute | solution.py:29
  144.2 54.1 %all-to-all-start.1 = ((f32[2,1,2048,128]{3,1,0,2:T(1,128)}), f32[2,1,2048,128]{3,1,0,2:T(1,128)}, u32[]{:S(2)}, u32[]{:S(2)}) async-start(f32[2,1,2048,128]{3,1,0,2:T(1,128)} %copy.369), calls=%async_computation.1 | async-start | bytes 4194304 | tf_op jit(solution)/shard_map/while/body/eval_jaxpr/all_to_all | solution.py:151
  198.3 52.2 %all-to-all-start = ((f32[2,1,2048,128]{3,1,0,2:T(1,128)}), f32[2,1,2048,128]{3,1,0,2:T(1,128)S(1)}, u32[]{:S(2)}, u32[]{:S(2)}) async-start(f32[2,1,2048,128]{3,1,0,2:T(1,128)} %copy.362), calls=%async_computation | async-start | bytes 4194304 | tf_op jit(solution)/shard_map/while/body/eval_jaxpr/all_to_all | solution.py:151
  203.1 73.6 %all-gather.6.cloned.1.call-start = ((), (), s32[]{:S(2)}) async-start(), calls=%async_computation.2 | async-start | bytes 1572864 | tf_op jit(solution)/shard_map/while/body/eval_jaxpr/all_gather | solution.py:131
  300.6 51.5 %collective-permute-start.5 = (f32[2,1,128,128]{3,2,0,1:T(8,128)}, f32[2,1,128,128]{3,2,0,1:T(8,128)}, u32[]{:S(2)}, u32[]{:S(2)}) collective-permute-start(f32[2,1,128,128]{3,2,0,1:T(8,128)} %get-tuple-element.399), channel_id=1, source_target_pairs={{0,6},{1,7},{2,8},{3,9},{4,10},{5,11},{6,12},{7,13},{8,14},{9,15},... | collective-permute-start | bytes 393224 | tf_op jit(solution)/shard_map/while/body/eval_jaxpr/ppermute | solution.py:29
  301.5 30.4 %collective-permute-start = (f32[2,1,128,128]{3,2,0,1:T(8,128)}, f32[2,1,128,128]{3,2,0,1:T(8,128)}, u32[]{:S(2)}, u32[]{:S(2)}) collective-permute-start(f32[2,1,128,128]{3,2,0,1:T(8,128)} %get-tuple-element.394), channel_id=1, source_target_pairs={{0,1},{1,2},{2,3},{3,4},{4,5},{5,6},{6,7},{7,8},{8,9},{9,10},{10,1... | collective-permute-start | bytes 393224 | tf_op jit(solution)/shard_map/while/body/eval_jaxpr/ppermute | solution.py:29
  304.1 31.3 %collective-permute-start.1 = (f32[2,1,128,128]{3,2,0,1:T(8,128)}, f32[2,1,128,128]{3,2,0,1:T(8,128)}, u32[]{:S(2)}, u32[]{:S(2)}) collective-permute-start(f32[2,1,128,128]{3,2,0,1:T(8,128)} %get-tuple-element.395), channel_id=1, source_target_pairs={{0,2},{1,3},{2,4},{3,5},{4,6},{5,7},{6,8},{7,9},{8,10},{9,11},{10,... | collective-permute-start | bytes 393224 | tf_op jit(solution)/shard_map/while/body/eval_jaxpr/ppermute | solution.py:29
  304.1 33.8 %collective-permute-start.2 = (f32[2,1,128,128]{3,2,0,1:T(8,128)}, f32[2,1,128,128]{3,2,0,1:T(8,128)}, u32[]{:S(2)}, u32[]{:S(2)}) collective-permute-start(f32[2,1,128,128]{3,2,0,1:T(8,128)} %get-tuple-element.396), channel_id=1, source_target_pairs={{0,3},{1,4},{2,5},{3,6},{4,7},{5,8},{6,9},{7,10},{8,11},{9,12},{10... | collective-permute-start | bytes 393224 | tf_op jit(solution)/shard_map/while/body/eval_jaxpr/ppermute | solution.py:29
  304.1 36.0 %collective-permute-start.3 = (f32[2,1,128,128]{3,2,0,1:T(8,128)}, f32[2,1,128,128]{3,2,0,1:T(8,128)}, u32[]{:S(2)}, u32[]{:S(2)}) collective-permute-start(f32[2,1,128,128]{3,2,0,1:T(8,128)} %get-tuple-element.397), channel_id=1, source_target_pairs={{0,4},{1,5},{2,6},{3,7},{4,8},{5,9},{6,10},{7,11},{8,12},{9,13},{1... | collective-permute-start | bytes 393224 | tf_op jit(solution)/shard_map/while/body/eval_jaxpr/ppermute | solution.py:29
  422.7 57.5 %all-to-all-start.1 = ((f32[2,1,2048,128]{3,1,0,2:T(1,128)}), f32[2,1,2048,128]{3,1,0,2:T(1,128)}, u32[]{:S(2)}, u32[]{:S(2)}) async-start(f32[2,1,2048,128]{3,1,0,2:T(1,128)} %copy.369), calls=%async_computation.1 | async-start | bytes 4194304 | tf_op jit(solution)/shard_map/while/body/eval_jaxpr/all_to_all | solution.py:151
  480.3 52.2 %all-to-all-start = ((f32[2,1,2048,128]{3,1,0,2:T(1,128)}), f32[2,1,2048,128]{3,1,0,2:T(1,128)S(1)}, u32[]{:S(2)}, u32[]{:S(2)}) async-start(f32[2,1,2048,128]{3,1,0,2:T(1,128)} %copy.362), calls=%async_computation | async-start | bytes 4194304 | tf_op jit(solution)/shard_map/while/body/eval_jaxpr/all_to_all | solution.py:151
  485.0 73.8 %all-gather.6.cloned.1.call-start = ((), (), s32[]{:S(2)}) async-start(), calls=%async_computation.2 | async-start | bytes 1572864 | tf_op jit(solution)/shard_map/while/body/eval_jaxpr/all_gather | solution.py:131
  582.6 51.8 %collective-permute-start.5 = (f32[2,1,128,128]{3,2,0,1:T(8,128)}, f32[2,1,128,128]{3,2,0,1:T(8,128)}, u32[]{:S(2)}, u32[]{:S(2)}) collective-permute-start(f32[2,1,128,128]{3,2,0,1:T(8,128)} %get-tuple-element.399), channel_id=1, source_target_pairs={{0,6},{1,7},{2,8},{3,9},{4,10},{5,11},{6,12},{7,13},{8,14},{9,15},... | collective-permute-start | bytes 393224 | tf_op jit(solution)/shard_map/while/body/eval_jaxpr/ppermute | solution.py:29
  583.5 30.6 %collective-permute-start = (f32[2,1,128,128]{3,2,0,1:T(8,128)}, f32[2,1,128,128]{3,2,0,1:T(8,128)}, u32[]{:S(2)}, u32[]{:S(2)}) collective-permute-start(f32[2,1,128,128]{3,2,0,1:T(8,128)} %get-tuple-element.394), channel_id=1, source_target_pairs={{0,1},{1,2},{2,3},{3,4},{4,5},{5,6},{6,7},{7,8},{8,9},{9,10},{10,1... | collective-permute-start | bytes 393224 | tf_op jit(solution)/shard_map/while/body/eval_jaxpr/ppermute | solution.py:29
  586.1 31.5 %collective-permute-start.1 = (f32[2,1,128,128]{3,2,0,1:T(8,128)}, f32[2,1,128,128]{3,2,0,1:T(8,128)}, u32[]{:S(2)}, u32[]{:S(2)}) collective-permute-start(f32[2,1,128,128]{3,2,0,1:T(8,128)} %get-tuple-element.395), channel_id=1, source_target_pairs={{0,2},{1,3},{2,4},{3,5},{4,6},{5,7},{6,8},{7,9},{8,10},{9,11},{10,... | collective-permute-start | bytes 393224 | tf_op jit(solution)/shard_map/while/body/eval_jaxpr/ppermute | solution.py:29
  586.1 34.0 %collective-permute-start.2 = (f32[2,1,128,128]{3,2,0,1:T(8,128)}, f32[2,1,128,128]{3,2,0,1:T(8,128)}, u32[]{:S(2)}, u32[]{:S(2)}) collective-permute-start(f32[2,1,128,128]{3,2,0,1:T(8,128)} %get-tuple-element.396), channel_id=1, source_target_pairs={{0,3},{1,4},{2,5},{3,6},{4,7},{5,8},{6,9},{7,10},{8,11},{9,12},{10... | collective-permute-start | bytes 393224 | tf_op jit(solution)/shard_map/while/body/eval_jaxpr/ppermute | solution.py:29
  586.1 36.2 %collective-permute-start.3 = (f32[2,1,128,128]{3,2,0,1:T(8,128)}, f32[2,1,128,128]{3,2,0,1:T(8,128)}, u32[]{:S(2)}, u32[]{:S(2)}) collective-permute-start(f32[2,1,128,128]{3,2,0,1:T(8,128)} %get-tuple-element.397), channel_id=1, source_target_pairs={{0,4},{1,5},{2,6},{3,7},{4,8},{5,9},{6,10},{7,11},{8,12},{9,13},{1... | collective-permute-start | bytes 393224 | tf_op jit(solution)/shard_map/while/body/eval_jaxpr/ppermute | solution.py:29
  704.9 57.5 %all-to-all-start.1 = ((f32[2,1,2048,128]{3,1,0,2:T(1,128)}), f32[2,1,2048,128]{3,1,0,2:T(1,128)}, u32[]{:S(2)}, u32[]{:S(2)}) async-start(f32[2,1,2048,128]{3,1,0,2:T(1,128)} %copy.369), calls=%async_computation.1 | async-start | bytes 4194304 | tf_op jit(solution)/shard_map/while/body/eval_jaxpr/all_to_all | solution.py:151
  762.4 52.2 %all-to-all-start = ((f32[2,1,2048,128]{3,1,0,2:T(1,128)}), f32[2,1,2048,128]{3,1,0,2:T(1,128)S(1)}, u32[]{:S(2)}, u32[]{:S(2)}) async-start(f32[2,1,2048,128]{3,1,0,2:T(1,128)} %copy.362), calls=%async_computation | async-start | bytes 4194304 | tf_op jit(solution)/shard_map/while/body/eval_jaxpr/all_to_all | solution.py:151
  767.2 73.8 %all-gather.6.cloned.1.call-start = ((), (), s32[]{:S(2)}) async-start(), calls=%async_computation.2 | async-start | bytes 1572864 | tf_op jit(solution)/shard_map/while/body/eval_jaxpr/all_gather | solution.py:131
  (90 other events, 810.8 us)
Sparse Core Ops, SparseCore 0:
  205.5 21.7 all-gather.5
  487.4 21.7 all-gather.5
  769.5 21.7 all-gather.5
